TPU v7x, 32 devices: a whole 2x2x4 slice. The times are simulated.
32 devices in a mesh: rows: 8 (over z, y), ch: 4 (over x, core).
Axes of the slice: x: 2, y: 2, z: 4, core: 2. Of those that a mesh axis runs over, the one named last changes fastest.
Arguments:
- tile_image: bfloat16 [768, 256, 256], P('ch', 'rows'), may hold values from -23 to 23
- spectral_filter: float32 [2, 768, 256, 256], P(None, 'ch', 'rows'), may hold values from -4 to 4
- conv_taps: float32 [768, 9], P('ch'), may hold values from -4 to 4
- norm_gain: float32 [768], replicated, may hold values from 0.25 to 1.75
- up_weight: bfloat16 [768, 3072], P(None, 'ch'), may hold values from -0.21875 to 0.21875
- down_weight: bfloat16 [3072, 768], P('ch'), may hold values from -0.109375 to 0.109375
- upstream: bfloat16 [768, 256, 256], P('ch', 'rows'), may hold values from -5 to 5
Outputs:
- block_out: bfloat16 [768, 256, 256], P('ch', 'rows')
- grad_image: float32 [768, 256, 256], P('ch', 'rows')
- grad_filter: float32 [2, 768, 256, 256], P(None, 'ch', 'rows')
All inputs are finite; a program needn't handle non-finite values.
Results may differ from a plain program's by a relative error of at most 0.012.
Values may be sent and summed in bfloat16 or wider, within the bound.
A program may use at most 192 MiB of HBM per device.

v0:
```python
import math
import jax
import jax.numpy as jnp
from jax import lax
from jax.sharding import PartitionSpec as P

norm_epsilon = 1e-05
root_half = 0.7071067811865476
density = 0.3989422804014327


def with_halo(block, sides, width):
    for axis, dim in sides:
        count = lax.axis_size(axis)
        forward = [(i, i + 1) for i in range(count - 1)]
        backward = [(target, source) for source, target in forward]
        low = lax.ppermute(
            lax.slice_in_dim(block, block.shape[dim] - width, None, axis=dim), axis, forward
        )
        high = lax.ppermute(lax.slice_in_dim(block, 0, width, axis=dim), axis, backward)
        block = jnp.concatenate([low, block, high], axis=dim)
    return block


def contract(form, left, right):
    return jnp.einsum(
        form, left, right, precision=lax.Precision.HIGHEST, preferred_element_type=jnp.float32
    )


def angle_tables(length):
    indices = jnp.arange(length, dtype=jnp.int32)
    products = indices[:, None] * indices[None, :] % length
    angles = products.astype(jnp.float32) * (2.0 * math.pi / length)
    return (jnp.cos(angles), jnp.sin(angles))


def filter_pass(signal, kernel_re, kernel_im):
    col_len = signal.shape[2]
    cos_w, sin_w = angle_tables(col_len)
    head_re = contract("chw,kw->ckh", signal, cos_w)
    head_im = -contract("chw,kw->ckh", signal, sin_w)
    col_re, col_im = (
        lax.all_to_all(
            head_re.astype(jnp.bfloat16), "rows", split_axis=1, concat_axis=2, tiled=True
        ).astype(head_re.dtype),
        lax.all_to_all(
            head_im.astype(jnp.bfloat16), "rows", split_axis=1, concat_axis=2, tiled=True
        ).astype(head_im.dtype),
    )
    row_len = col_re.shape[2]
    cos_h, sin_h = angle_tables(row_len)
    spec_re = contract("cwh,kh->cwk", col_re, cos_h) + contract("cwh,kh->cwk", col_im, sin_h)
    spec_im = contract("cwh,kh->cwk", col_im, cos_h) - contract("cwh,kh->cwk", col_re, sin_h)
    prod_re = kernel_re * spec_re - kernel_im * spec_im
    prod_im = kernel_re * spec_im + kernel_im * spec_re
    back_re = contract("cwk,kh->cwh", prod_re, cos_h) - contract("cwk,kh->cwh", prod_im, sin_h)
    back_im = contract("cwk,kh->cwh", prod_im, cos_h) + contract("cwk,kh->cwh", prod_re, sin_h)
    row_re, row_im = (
        lax.all_to_all(
            back_re.astype(jnp.bfloat16), "rows", split_axis=2, concat_axis=1, tiled=True
        ).astype(back_re.dtype),
        lax.all_to_all(
            back_im.astype(jnp.bfloat16), "rows", split_axis=2, concat_axis=1, tiled=True
        ).astype(back_im.dtype),
    )
    outcome = contract("ckh,kw->chw", row_re, cos_w) - contract("ckh,kw->chw", row_im, sin_w)
    return (outcome * (1.0 / (row_len * col_len)), spec_re, spec_im)


def depthwise(signal, tap_weights):
    token_row_count, col_count = (signal.shape[1], signal.shape[2])
    padded = with_halo(signal.astype(jnp.bfloat16), (("rows", 1),), 1).astype(signal.dtype)
    padded = jnp.pad(padded, ((0, 0), (0, 0), (1, 1)))
    running = jnp.zeros_like(signal)
    for row_off in range(3):
        for col_off in range(3):
            running = (
                running
                + tap_weights[:, 3 * row_off + col_off][:, None, None]
                * padded[:, row_off : row_off + token_row_count, col_off : col_off + col_count]
            )
    return running


def layer_norm(whole):
    values = whole.astype(jnp.float32)
    centred = values - jnp.mean(values, axis=0)[None]
    inv_std = lax.rsqrt(jnp.mean(centred * centred, axis=0) + norm_epsilon)
    return (centred * inv_std[None], inv_std)


def gelu_slope(pre_act):
    return 0.5 * (1.0 + lax.erf(pre_act * root_half)) + pre_act * density * jnp.exp(
        -0.5 * pre_act * pre_act
    )


def norm_back(normed_gradient, normed, inv_std, gain):
    weighted = normed_gradient * gain[None, :, None, None]
    mean_one = jnp.mean(weighted, axis=1, keepdims=True)
    second = jnp.mean(weighted * normed[None], axis=1, keepdims=True)
    return inv_std[None, None] * (weighted - mean_one - normed[None] * second)


def settle(partials):
    return jnp.sum(
        lax.optimization_barrier(partials.astype(jnp.bfloat16)).astype(jnp.float32), axis=0
    )


def to_tokens(values):
    return lax.all_to_all(values, "ch", split_axis=2, concat_axis=0, tiled=True)


def to_channels(values):
    return lax.all_to_all(
        values.astype(jnp.bfloat16), "ch", split_axis=0, concat_axis=2, tiled=True
    ).astype(values.dtype)


def on_device(tile_image, spectral_filter, conv_taps, norm_gain, up_weight, down_weight, upstream):
    signal = tile_image.astype(jnp.float32)
    filtered, spec_re, spec_im = filter_pass(signal, spectral_filter[0], spectral_filter[1])
    hidden_state = signal + depthwise(filtered, conv_taps)
    rounded = hidden_state.astype(jnp.bfloat16)
    gain_column = norm_gain[:, None, None]
    full_up, full_down = (
        lax.all_gather(up_weight, "ch", axis=1, tiled=True),
        lax.all_gather(down_weight, "ch", axis=0, tiled=True),
    )
    blocks = lax.axis_size("ch")
    channels, hidden_units = (full_up.shape[0], full_up.shape[1])
    hidden_share_units = hidden_units // blocks
    normed, inv_std = layer_norm(to_tokens(rounded))
    scaled = (normed * gain_column).astype(jnp.bfloat16)
    pre_act = jnp.einsum("chw,cf->fhw", scaled, full_up, preferred_element_type=jnp.float32)
    activated = jax.nn.gelu(pre_act, approximate=False).astype(jnp.bfloat16)
    token_row_count, col_count = (activated.shape[1], activated.shape[2])
    partials = jnp.einsum(
        "bfhw,bfc->bchw",
        activated.reshape(blocks, hidden_share_units, token_row_count, col_count),
        full_down.reshape(blocks, hidden_share_units, channels),
        preferred_element_type=jnp.float32,
    )
    out_sum = to_channels(settle(partials))
    block_out = (hidden_state + out_sum).astype(jnp.bfloat16)
    whole_dy = to_tokens(upstream)
    grad_act = jnp.einsum("chw,fc->fhw", whole_dy, full_down, preferred_element_type=jnp.float32)
    preactivation_gradient = (grad_act * gelu_slope(pre_act)).astype(jnp.bfloat16)
    normed_gradient = jnp.einsum(
        "pjra,spj->psra",
        preactivation_gradient.reshape(blocks, hidden_share_units, token_row_count, col_count),
        full_up.reshape(channels, blocks, hidden_share_units),
        preferred_element_type=jnp.float32,
    )
    grad_mlp = to_channels(settle(norm_back(normed_gradient, normed, inv_std, norm_gain)))
    grad_hidden = upstream.astype(jnp.float32) + grad_mlp
    grad_filtered = depthwise(grad_hidden, conv_taps[:, ::-1])
    adjoint, grad_re, grad_im = filter_pass(grad_filtered, spectral_filter[0], -spectral_filter[1])
    grad_image = grad_hidden + adjoint
    factor = 1.0 / (tile_image.shape[2] * spec_re.shape[2])
    grad_filter = jnp.stack(
        [
            (grad_re * spec_re + grad_im * spec_im) * factor,
            (grad_im * spec_re - grad_re * spec_im) * factor,
        ]
    )
    return (block_out, grad_image, grad_filter)


def solution(mesh):
    return jax.shard_map(
        on_device,
        mesh=mesh,
        in_specs=(
            P("ch", "rows", None),
            P(None, "ch", "rows", None),
            P("ch", None),
            P(),
            P(None, "ch"),
            P("ch", None),
            P("ch", "rows", None),
        ),
        out_specs=(P("ch", "rows", None), P("ch", "rows", None), P(None, "ch", "rows", None)),
        check_vma=False,
    )
```

profile of v0, /device:TPU:0, one launch (start us, length us, event | category | flops | bytes accessed | tf_op | source)
XLA Modules:
  0.0 1455.8 jit_solution(15047290855060164912)
XLA Ops:
  7.2 10.0 fusion.76
  48.6 77.4 %all-to-all-done.1 = bf16[192,256,32]{0,2,1:T(8,128)(2,1)} async-done(((bf16[192,256,32]{0,2,1:T(8,128)(2,1)}), bf16[192,256,32]{0,2,1:T(8,128)(2,1)}, u32[]{:S(2)}, u32[]{:S(2)}) %all-to-all-start.1) | async-done | bytes 3145760 | tf_op jit(solution)/shard_map/all_to_all | solution.py:47
  148.3 75.1 %all-to-all-done = bf16[192,256,32]{0,2,1:T(8,128)(2,1)} async-done(((bf16[192,256,32]{0,2,1:T(8,128)(2,1)}), bf16[192,256,32]{0,2,1:T(8,128)(2,1)}, u32[]{:S(2)}, u32[]{:S(2)}) %all-to-all-start) | async-done | bytes 3145760 | tf_op jit(solution)/shard_map/all_to_all | solution.py:44
  250.1 15.3 %fusion.64 = (f32[192,32,256]{2,1,0:T(8,128)}, f32[192,32,256]{2,1,0:T(8,128)}, f32[192,32,256]{2,1,0:T(8,128)}) fusion(f32[192,32,256]{2,1,0:T(8,128)} %convolution_subtract_fusion.1, f32[2,192,32,256]{3,2,1,0:T(8,128)} %param.8, f32[192,32,256]{2,1,0:T(8,128)} %fusion.125, bf16[192,32,256]{2,1,0:T(8,128)(2,1)S(1)} %copy.223), kind=kOutput, calls=%fused_computation.102 | convolution fusion | flops 4843765760 | bytes 47185920 | tf_op jit(solution)/shard_map/cwh,kh->cwk/dot_general | solution.py:26
  265.4 10.9 fusion.121
  295.4 10.9 fusion.117
  323.2 64.0 %all-to-all-done.2 = bf16[192,32,256]{0,1,2:T(8,128)(2,1)} async-done(((bf16[192,32,256]{0,1,2:T(8,128)(2,1)}), bf16[192,32,256]{0,1,2:T(8,128)(2,1)}, u32[]{:S(2)}, u32[]{:S(2)}) %all-to-all-start.2) | async-done | bytes 3145760 | tf_op jit(solution)/shard_map/all_to_all | solution.py:60
  413.3 71.0 %all-to-all-done.3 = bf16[192,32,256]{0,1,2:T(8,128)(2,1)} async-done(((bf16[192,32,256]{0,1,2:T(8,128)(2,1)}), bf16[192,32,256]{0,1,2:T(8,128)(2,1)}, u32[]{:S(2)}, u32[]{:S(2)}) %all-to-all-start.3) | async-done | bytes 3145760 | tf_op jit(solution)/shard_map/all_to_all | solution.py:63
  530.1 37.9 %fusion.253 = (bf16[192,32,256]{2,1,0:T(8,128)(2,1)S(1)}, f32[192,32,256]{2,1,0:T(8,128)}) fusion(f32[192]{0:T(256)S(1)} %bitcast.308, f32[192,34,256]{2,1,0:T(8,128)} %maximum_convert_fusion, f32[192]{0:T(256)S(1)} %bitcast.310, f32[192]{0:T(256)S(1)} %bitcast.296, f32[192]{0:T(256)S(1)} %bitcast.298, f32[192]{0:T(256)S(1)} %bitcast.300, ...), kind=kLoop, calls=%fused_computation.292 | loop fusion | flops 31457280 | bytes 39328512 | tf_op jit(solution)/shard_map/convert_element_type | solution.py:126
  593.7 9.8 reshape.83
  603.5 16.1 %fusion.261 = f32[3072,2048]{0,1} fusion(bf16[3072,768]{1,0:T(8,128)(2,1)} %all-gather.5.cloned.1.call-done, bf16[768,2048]{0,1:T(8,128)(2,1)S(1)} %reshape.95), kind=kOutput, calls=%fused_computation.297 | convolution fusion | flops 9663676416 | bytes 33030144
  627.4 9.6 fusion.255
  637.1 13.8 copy.236
  650.9 10.2 reshape.84
  669.5 80.0 %fusion.7 = (bf16[3072,32,64]{0,2,1:T(8,128)(2,1)}, bf16[3072,32,64]{0,2,1:T(8,128)(2,1)}) fusion(f32[3072,32,64]{0,2,1:T(8,128)} %bitcast.313, bf16[768,3072]{1,0:T(8,128)(2,1)S(1)} %bitcast.292, f32[768,32,64]{0,2,1:T(8,128)S(1)} %subtract_multiply_fusion, f32[768]{0:T(1024)S(1)} %copy-done.33), kind=kOutput, calls=%fused_computation.9 | convolution fusion | flops 10138681344 | bytes 61344768 | tf_op jit(solution)/shard_map/chw,cf->fhw/dot_general | solution.py:137
  749.4 22.7 %bitcast_reduce_fusion = (f32[4,32,64]{2,1,0:T(8,128)S(1)}, f32[4,32,64]{2,1,0:T(8,128)S(1)}, f32[4,32,64,768]{3,2,1,0:T(8,128)}) fusion(f32[768]{0:T(1024)S(1)} %copy-done.33, f32[768,32,64]{0,2,1:T(8,128)} %copy-done.9, bf16[768,4,768,1]{2,1,0,3:T(4,128)(2,1)} %bitcast.293, bf16[32,8,4,8,768]{4,3,2,1,0:T(8,128)(2,1)} %bitcast.315), kind=kOutput, calls=%fused_computation.12 | convolution fusion | flops 9688825856 | bytes 48827392 | tf_op jit(solution)/shard_map/pjra,spj->psra/dot_general | solution.py:151
  772.2 16.0 %fusion.10 = bf16[4,768,32,64]{1,3,2,0:T(8,128)(2,1)} fusion(f32[4,32,64,768]{3,2,1,0:T(8,128)} %get-tuple-element.33, f32[4,32,64]{2,1,0:T(8,128)S(1)} %get-tuple-element.34, f32[768,32,64]{0,2,1:T(8,128)} %copy-done.9, f32[4,32,64]{2,1,0:T(8,128)S(1)} %get-tuple-element.35, f32[768]{0:T(1024)S(1)} %copy-done.33, f32[32,64]{1,0:T(8,128)S(1)} %copy-done.13), kind=kLoop, calls=%fused_computation.15 | loop fusion | flops 37748736 | bytes 44116992 | tf_op jit(solution)/shard_map/convert_element_type | solution.py:108
  795.5 9.7 copy.247
  811.7 40.3 %all_to_all.189 = bf16[4,2,196608]{2,1,0:T(2,128)(2,1)} all-to-all(bf16[4,2,196608]{2,1,0:T(2,128)(2,1)S(1)} %reshape.101), channel_id=1, replica_groups=mesh['rows'=8,'ch'=4] {'ch'}, dimensions={0} | all-to-all | bytes 6291456 | tf_op jit(solution)/shard_map/all_to_all | solution.py:117
  912.3 15.1 %fusion.57 = f32[192,32,256]{2,1,0:T(8,128)} fusion(f32[192,34,256]{2,1,0:T(8,128)S(1)} %maximum_convert_fusion.1, f32[192]{0:T(256)S(1)} %bitcast.309, f32[192]{0:T(256)S(1)} %bitcast.311, f32[192]{0:T(256)S(1)} %bitcast.297, f32[192]{0:T(256)S(1)} %bitcast.299, f32[192]{0:T(256)S(1)} %bitcast.301, f32[192]{0:T(256)S(1)} %bitcast.303, f32[192]{0:T(256)S(1)} %bitcast.305, ...), kind=kLoop, calls=%fused_computation.86 | loop fusion | flops 26738688 | bytes 33039360 | tf_op jit(solution)/shard_map/add | solution.py:79
  927.4 12.5 fusion.77
  950.5 12.5 convert_bitcast_fusion.2
  968.7 75.3 %all-to-all-done.9 = bf16[192,256,32]{0,2,1:T(8,128)(2,1)} async-done(((bf16[192,256,32]{0,2,1:T(8,128)(2,1)}), bf16[192,256,32]{0,2,1:T(8,128)(2,1)}, u32[]{:S(2)}, u32[]{:S(2)}) %all-to-all-start.9) | async-done | bytes 3145760 | tf_op jit(solution)/shard_map/all_to_all | solution.py:47
  1048.9 17.0 %convert_bitcast_fusion = bf16[4,768,32,64]{1,3,2,0:T(8,128)(2,1)} fusion(bf16[4,768,768,1]{2,1,3,0:T(8,128)(2,1)} %bitcast.312, bf16[32,8,4,8,768]{4,3,2,1,0:T(8,128)(2,1)} %bitcast.314), kind=kOutput, calls=%fused_computation.60 | convolution fusion | flops 9669967872 | bytes 29884416 | tf_op jit(solution)/shard_map/bfhw,bfc->bchw/dot_general | solution.py:140
  1107.7 33.9 %all-to-all-done.8 = bf16[192,256,32]{0,2,1:T(8,128)(2,1)} async-done(((bf16[192,256,32]{0,2,1:T(8,128)(2,1)}), bf16[192,256,32]{0,2,1:T(8,128)(2,1)}, u32[]{:S(2)}, u32[]{:S(2)}) %all-to-all-start.8) | async-done | bytes 3145760 | tf_op jit(solution)/shard_map/all_to_all | solution.py:44
  1176.4 23.1 %multiply_bitcast_fusion.1 = (f32[1,192,32,256]{3,2,1,0:T(8,128)}, f32[1,192,32,256]{3,2,1,0:T(8,128)}, f32[192,32,256]{2,1,0:T(8,128)}, f32[192,32,256]{2,1,0:T(8,128)}) fusion(f32[192,32,256]{2,1,0:T(8,128)} %convolution_subtract_fusion, f32[192,32,256]{2,1,0:T(8,128)S(1)} %bitcast.270, f32[192,32,256]{2,1,0:T(8,128)} %get-tuple-element.32, ...), kind=kOutput, calls=%fused_computation.110 | convolution fusion | flops 4857921536 | bytes 66060288 | tf_op jit(solution)/shard_map/cwh,kh->cwk/dot_general | solution.py:26
  1199.6 11.1 fusion.110
  1229.3 10.9 fusion.106
  1257.0 66.3 %all-to-all-done.10 = bf16[192,32,256]{0,1,2:T(8,128)(2,1)} async-done(((bf16[192,32,256]{0,1,2:T(8,128)(2,1)}), bf16[192,32,256]{0,1,2:T(8,128)(2,1)}, u32[]{:S(2)}, u32[]{:S(2)}) %all-to-all-start.10) | async-done | bytes 3145760 | tf_op jit(solution)/shard_map/all_to_all | solution.py:60
  1375.8 9.7 pad_maximum_fusion
  1406.4 15.1 %all-to-all-done.11 = bf16[192,32,256]{0,1,2:T(8,128)(2,1)} async-done(((bf16[192,32,256]{0,1,2:T(8,128)(2,1)}), bf16[192,32,256]{0,1,2:T(8,128)(2,1)}, u32[]{:S(2)}, u32[]{:S(2)}) %all-to-all-start.11) | async-done | bytes 3145760 | tf_op jit(solution)/shard_map/all_to_all | solution.py:63
  1436.8 12.0 multiply_add_fusion
  (191 shorter events, 525.4 us)
Async XLA Ops:
  24.9 101.1 %all-to-all-start.1 = ((bf16[192,256,32]{0,2,1:T(8,128)(2,1)}), bf16[192,256,32]{0,2,1:T(8,128)(2,1)}, u32[]{:S(2)}, u32[]{:S(2)}) async-start(bf16[192,256,32]{0,2,1:T(8,128)(2,1)} %copy.221), calls=%async_computation.1 | async-start | bytes 8388608 | tf_op jit(solution)/shard_map/all_to_all | solution.py:47
  126.0 97.3 %all-to-all-start = ((bf16[192,256,32]{0,2,1:T(8,128)(2,1)}), bf16[192,256,32]{0,2,1:T(8,128)(2,1)}, u32[]{:S(2)}, u32[]{:S(2)}) async-start(bf16[192,256,32]{0,2,1:T(8,128)(2,1)} %copy.217), calls=%async_computation | async-start | bytes 8388608 | tf_op jit(solution)/shard_map/all_to_all | solution.py:44
  290.1 97.1 %all-to-all-start.2 = ((bf16[192,32,256]{0,1,2:T(8,128)(2,1)}), bf16[192,32,256]{0,1,2:T(8,128)(2,1)}, u32[]{:S(2)}, u32[]{:S(2)}) async-start(bf16[192,32,256]{0,1,2:T(8,128)(2,1)} %copy.226), calls=%async_computation.2 | async-start | bytes 8388608 | tf_op jit(solution)/shard_map/all_to_all | solution.py:60
  294.7 299.0 %all-gather.3.cloned.1.call-start = ((), (), s32[]{:S(2)}) async-start(), calls=%async_computation.12 | async-start | bytes 5898240 | tf_op jit(solution)/shard_map/all_gather | solution.py:129
  323.2 69.3 %copy-start.3 = (bf16[192,32,256]{2,1,0:T(8,128)(2,1)S(1)}, bf16[192,32,256]{2,1,0:T(8,128)(2,1)}, u32[]{:S(2)}) copy-start(bf16[192,32,256]{2,1,0:T(8,128)(2,1)} %param.13) | copy-start | bytes 9437188
  387.2 97.1 %all-to-all-start.3 = ((bf16[192,32,256]{0,1,2:T(8,128)(2,1)}), bf16[192,32,256]{0,1,2:T(8,128)(2,1)}, u32[]{:S(2)}, u32[]{:S(2)}) async-start(bf16[192,32,256]{0,1,2:T(8,128)(2,1)} %copy.230), calls=%async_computation.3 | async-start | bytes 8388608 | tf_op jit(solution)/shard_map/all_to_all | solution.py:63
  391.8 211.7 %all-gather.5.cloned.1.call-start = ((), (), s32[]{:S(2)}) async-start(), calls=%async_computation.13 | async-start | bytes 5898240 | tf_op jit(solution)/shard_map/all_gather | solution.py:130
  484.3 90.1 %all-to-all-start.6 = ((bf16[192,32,256]{0,1,2:T(8,128)(2,1)}), bf16[192,32,256]{0,1,2:T(8,128)(2,1)}, u32[]{:S(2)}, u32[]{:S(2)}) async-start(bf16[192,32,256]{0,1,2:T(8,128)(2,1)} %copy.242), calls=%async_computation.6 | async-start | bytes 8388608 | tf_op jit(solution)/shard_map/all_to_all | solution.py:113
  512.5 9.2 collective-permute-start.1
  513.8 12.0 collective-permute-start
  518.6 49.4 %copy-start.14 = (f32[192,1]{0,1:T(1,128)}, f32[192,1]{0,1:T(1,128)S(1)}, u32[]{:S(2)}) copy-start(f32[192,1]{0,1:T(1,128)S(1)} %get-tuple-element.23) | copy-start | bytes 2308
  518.6 49.4 %copy-start.16 = (f32[192,1]{0,1:T(1,128)}, f32[192,1]{0,1:T(1,128)S(1)}, u32[]{:S(2)}) copy-start(f32[192,1]{0,1:T(1,128)S(1)} %get-tuple-element.24) | copy-start | bytes 2308
  518.6 49.4 %copy-start.18 = (f32[192,1]{0,1:T(1,128)}, f32[192,1]{0,1:T(1,128)S(1)}, u32[]{:S(2)}) copy-start(f32[192,1]{0,1:T(1,128)S(1)} %get-tuple-element.25) | copy-start | bytes 2308
  518.6 49.4 %copy-start.20 = (f32[192,1]{0,1:T(1,128)}, f32[192,1]{0,1:T(1,128)S(1)}, u32[]{:S(2)}) copy-start(f32[192,1]{0,1:T(1,128)S(1)} %get-tuple-element.26) | copy-start | bytes 2308
  518.6 49.4 %copy-start.22 = (f32[192,1]{0,1:T(1,128)}, f32[192,1]{0,1:T(1,128)S(1)}, u32[]{:S(2)}) copy-start(f32[192,1]{0,1:T(1,128)S(1)} %get-tuple-element.27) | copy-start | bytes 2308
  518.6 49.4 %copy-start.24 = (f32[192,1]{0,1:T(1,128)}, f32[192,1]{0,1:T(1,128)S(1)}, u32[]{:S(2)}) copy-start(f32[192,1]{0,1:T(1,128)S(1)} %get-tuple-element.28) | copy-start | bytes 2308
  518.6 49.4 %copy-start.26 = (f32[192,1]{0,1:T(1,128)}, f32[192,1]{0,1:T(1,128)S(1)}, u32[]{:S(2)}) copy-start(f32[192,1]{0,1:T(1,128)S(1)} %get-tuple-element.29) | copy-start | bytes 2308
  518.6 49.4 %copy-start.28 = (f32[192,1]{0,1:T(1,128)}, f32[192,1]{0,1:T(1,128)S(1)}, u32[]{:S(2)}) copy-start(f32[192,1]{0,1:T(1,128)S(1)} %get-tuple-element.30) | copy-start | bytes 2308
  518.6 49.4 %copy-start.30 = (f32[192,1]{0,1:T(1,128)}, f32[192,1]{0,1:T(1,128)S(1)}, u32[]{:S(2)}) copy-start(f32[192,1]{0,1:T(1,128)S(1)} %get-tuple-element.31) | copy-start | bytes 2308
  574.4 53.1 %all-to-all-start.4 = ((bf16[192,32,256]{0,1,2:T(8,128)(2,1)}), bf16[192,32,256]{0,1,2:T(8,128)(2,1)}, u32[]{:S(2)}, u32[]{:S(2)}) async-start(bf16[192,32,256]{0,1,2:T(8,128)(2,1)} %copy.234), calls=%async_computation.4 | async-start | bytes 8388608 | tf_op jit(solution)/shard_map/all_to_all | solution.py:113
  669.4 80.0 %copy-start.9 = (f32[768,32,64]{0,2,1:T(8,128)}, f32[768,32,64]{0,2,1:T(8,128)S(1)}, u32[]{:S(2)}) copy-start(f32[768,32,64]{0,2,1:T(8,128)S(1)} %subtract_multiply_fusion) | copy-start | bytes 18874372
  749.4 22.7 %copy-start.13 = (f32[32,64]{1,0:T(8,128)S(1)}, f32[32,64]{1,0:T(8,128)}, u32[]{:S(2)}) copy-start(f32[32,64]{1,0:T(8,128)} %copy-done.12) | copy-start | bytes 24580
  895.8 16.4 %copy-start.15 = (f32[192,1]{0,1:T(1,128)S(1)}, f32[192,1]{0,1:T(1,128)}, u32[]{:S(2)}) copy-start(f32[192,1]{0,1:T(1,128)} %copy-done.14) | copy-start | bytes 2308
  896.2 8.9 collective-permute-start.3
  897.5 12.0 collective-permute-start.2
  945.7 98.4 %all-to-all-start.9 = ((bf16[192,256,32]{0,2,1:T(8,128)(2,1)}), bf16[192,256,32]{0,2,1:T(8,128)(2,1)}, u32[]{:S(2)}, u32[]{:S(2)}) async-start(bf16[192,256,32]{0,2,1:T(8,128)(2,1)} %copy.256), calls=%async_computation.9 | async-start | bytes 8388608 | tf_op jit(solution)/shard_map/all_to_all | solution.py:47
  1044.1 97.6 %all-to-all-start.8 = ((bf16[192,256,32]{0,2,1:T(8,128)(2,1)}), bf16[192,256,32]{0,2,1:T(8,128)(2,1)}, u32[]{:S(2)}, u32[]{:S(2)}) async-start(bf16[192,256,32]{0,2,1:T(8,128)(2,1)} %copy.252), calls=%async_computation.8 | async-start | bytes 8388608 | tf_op jit(solution)/shard_map/all_to_all | solution.py:44
  1141.6 82.8 %all-to-all-start.5 = ((bf16[4,2,196608]{2,1,0:T(2,128)(2,1)}), bf16[4,2,196608]{2,1,0:T(2,128)(2,1)}, u32[]{:S(2)}, u32[]{:S(2)}) async-start(bf16[4,2,196608]{2,1,0:T(2,128)(2,1)} %reshape.99), calls=%async_computation.5 | async-start | bytes 6291456 | tf_op jit(solution)/shard_map/all_to_all | solution.py:117
  1158.8 17.6 %slice-start = ((s8[6291456]{0:T(1024)(128)(4,1)}), s8[4194304]{0:T(1024)(128)(4,1)S(1)}, s32[]{:S(2)}) async-start(s8[6291456]{0:T(1024)(128)(4,1)} %bitcast.269), calls=%async_computation.14 | async-start | bytes 8388608
  1224.4 99.0 %all-to-all-start.10 = ((bf16[192,32,256]{0,1,2:T(8,128)(2,1)}), bf16[192,32,256]{0,1,2:T(8,128)(2,1)}, u32[]{:S(2)}, u32[]{:S(2)}) async-start(bf16[192,32,256]{0,1,2:T(8,128)(2,1)} %copy.261), calls=%async_computation.10 | async-start | bytes 8388608 | tf_op jit(solution)/shard_map/all_to_all | solution.py:60
  1323.4 98.2 %all-to-all-start.11 = ((bf16[192,32,256]{0,1,2:T(8,128)(2,1)}), bf16[192,32,256]{0,1,2:T(8,128)(2,1)}, u32[]{:S(2)}, u32[]{:S(2)}) async-start(bf16[192,32,256]{0,1,2:T(8,128)(2,1)} %copy.265), calls=%async_computation.11 | async-start | bytes 8388608 | tf_op jit(solution)/shard_map/all_to_all | solution.py:63
  1358.7 17.0 %slice-start.6 = ((s8[6291456]{0:T(1024)(128)(4,1)}), s8[2097152]{0:T(1024)(128)(4,1)S(1)}, s32[]{:S(2)}) async-start(s8[6291456]{0:T(1024)(128)(4,1)} %bitcast.281), calls=%async_computation.20 | async-start | bytes 4194304
  (29 other events, 317.1 us)
Sparse Core Ops, SparseCore 0:
  297.1 38.7 all-gather.2
  394.2 38.7 all-gather.4
where the time goes:
time: 1470 us; the launch traced here: 1460 us
  waiting for transfers between devices  501 us (34%)
  matrix products  365 us (25%)
  local copies, waits for them, and re-layouts  336 us (23%)
  other arithmetic  129 us (9%)
  starting transfers between devices  69.1 us (5%)
  blocking collectives  40.3 us (3%)
  between operations  15.2 us (1%)
    dot_general x24, matrix products, contract(): jnp.einsum(form, left, right, precision=lax.Precision.HIGHEST, preferred_...  229 us
    all_to_all x2, waiting for transfers between devices, filter_pass(): lax.all_to_all(head_im.astype(jnp.bfloat16), 'rows', split_axis=1, concat...  153 us
    all_to_all x2, waiting for transfers between devices, filter_pass(): lax.all_to_all(back_re.astype(jnp.bfloat16), 'rows', split_axis=2, concat...  130 us
    all_to_all x2, waiting for transfers between devices, filter_pass(): lax.all_to_all(head_re.astype(jnp.bfloat16), 'rows', split_axis=1, concat...  109 us
    all_to_all x2, waiting for transfers between devices, filter_pass(): lax.all_to_all(back_im.astype(jnp.bfloat16), 'rows', split_axis=2, concat...  86.2 us
    dot_general x1, matrix products, on_device(): jnp.einsum('chw,cf->fhw', scaled, full_up, preferred_element_type=jnp.flo...  80 us
    convert_element_type x6, local copies, waits for them, and re-layouts, to_channels(): return lax.all_to_all(values.astype(jnp.bfloat16), 'ch', split_axis=0, co...  50.7 us
    unnamed x94, local copies, waits for them, and re-layouts  43.1 us
  transfers between devices with their start and end apart: 17, of which 13 were waited for; matrix products, arithmetic and copies ran while one was open for 31% of the time, Pallas kernels for 0%

commit v1 on v0

--- a/solution.py
+++ b/solution.py
@@ -7,6 +7,29 @@
 norm_epsilon = 1e-05
 root_half = 0.7071067811865476
 density = 0.3989422804014327
+
+
+def cut_along(shard, dim, size):
+    shape = shard.shape
+    blocks = shard.reshape(*shape[:dim], size, shape[dim] // size, *shape[dim + 1 :])
+    return jnp.moveaxis(blocks, dim, 0)
+
+
+def in_order(parts, dim):
+    lengths = list(parts.shape[1:])
+    lengths[dim] *= parts.shape[0]
+    return jnp.moveaxis(parts, 0, dim).reshape(lengths)
+
+
+def rotated_exchange(x, axis, split_dim, concat_dim):
+    devices, mine = (lax.axis_size(axis), lax.axis_index(axis))
+    tiles = cut_along(x, split_dim, devices)
+    outs = [tiles[mine]]
+    for step in range(1, devices):
+        sent = tiles[(mine + step) % devices]
+        outs.append(lax.ppermute(sent, axis, [(i, (i + step) % devices) for i in range(devices)]))
+    tiles = jnp.stack(outs)[(mine - jnp.arange(devices)) % devices]
+    return in_order(tiles, concat_dim)
 
 
 def with_halo(block, sides, width):
@@ -60,9 +83,7 @@
         lax.all_to_all(
             back_re.astype(jnp.bfloat16), "rows", split_axis=2, concat_axis=1, tiled=True
         ).astype(back_re.dtype),
-        lax.all_to_all(
-            back_im.astype(jnp.bfloat16), "rows", split_axis=2, concat_axis=1, tiled=True
-        ).astype(back_im.dtype),
+        rotated_exchange(back_im.astype(jnp.bfloat16), "rows", 2, 1).astype(back_im.dtype),
     )
     outcome = contract("ckh,kw->chw", row_re, cos_w) - contract("ckh,kw->chw", row_im, sin_w)
     return (outcome * (1.0 / (row_len * col_len)), spec_re, spec_im)

time: 1470 us -> 1480 us (level)
  the two profiles are of different devices: /device:TPU:0 before, /device:TPU:31 now
where the time goes in v1:
time: 1480 us; the launch traced here: 1470 us
  waiting for transfers between devices  392 us (26%)
  matrix products  357 us (24%)
  local copies, waits for them, and re-layouts  355 us (24%)
  starting transfers between devices  180 us (12%)
  other arithmetic  132 us (9%)
  blocking collectives  40.3 us (3%)
  between operations  15.3 us (1%)
    dot_general x24, matrix products, contract(): jnp.einsum(form, left, right, precision=lax.Precision.HIGHEST, preferred_...  221 us
    all_to_all x2, waiting for transfers between devices, filter_pass(): lax.all_to_all(head_im.astype(jnp.bfloat16), 'rows', split_axis=1, concat...  149 us
    ppermute x14, starting transfers between devices, rotated_exchange(): lax.ppermute(sent, axis, [(i, (i + step) % devices) for i in range(device...  115 us
    all_to_all x2, waiting for transfers between devices, filter_pass(): lax.all_to_all(head_re.astype(jnp.bfloat16), 'rows', split_axis=1, concat...  113 us
    ppermute x14, waiting for transfers between devices, rotated_exchange(): lax.ppermute(sent, axis, [(i, (i + step) % devices) for i in range(device...  111 us
    dot_general x1, matrix products, on_device(): jnp.einsum('chw,cf->fhw', scaled, full_up, preferred_element_type=jnp.flo...  79.9 us
    unnamed x106, local copies, waits for them, and re-layouts  58.8 us
    convert_element_type x6, local copies, waits for them, and re-layouts, to_channels(): return lax.all_to_all(values.astype(jnp.bfloat16), 'ch', split_axis=0, co...  50.8 us
  transfers between devices with their start and end apart: 29, of which 13 were waited for; matrix products, arithmetic and copies ran while one was open for 36% of the time, Pallas kernels for 0%

profile of v1, /device:TPU:31, one launch (start us, length us, event | category | flops | bytes accessed | tf_op | source)
XLA Modules:
  0.0 1471.9 jit_solution(15930954526008901719)
XLA Ops:
  7.2 10.0 fusion.76
  46.7 75.8 %all-to-all-done.1 = bf16[192,256,32]{0,2,1:T(8,128)(2,1)} async-done(((bf16[192,256,32]{0,2,1:T(8,128)(2,1)}), bf16[192,256,32]{0,2,1:T(8,128)(2,1)}, u32[]{:S(2)}, u32[]{:S(2)}) %all-to-all-start.1) | async-done | bytes 3145760 | tf_op jit(solution)/shard_map/all_to_all | solution.py:70
  139.7 79.9 %all-to-all-done = bf16[192,256,32]{0,2,1:T(8,128)(2,1)} async-done(((bf16[192,256,32]{0,2,1:T(8,128)(2,1)}), bf16[192,256,32]{0,2,1:T(8,128)(2,1)}, u32[]{:S(2)}, u32[]{:S(2)}) %all-to-all-start) | async-done | bytes 3145760 | tf_op jit(solution)/shard_map/all_to_all | solution.py:67
  248.2 15.1 %fusion.64 = (f32[192,32,256]{2,1,0:T(8,128)}, f32[192,32,256]{2,1,0:T(8,128)}, f32[192,32,256]{2,1,0:T(8,128)}) fusion(f32[192,32,256]{2,1,0:T(8,128)} %convolution_subtract_fusion.1, f32[2,192,32,256]{3,2,1,0:T(8,128)} %param.8, f32[192,32,256]{2,1,0:T(8,128)} %fusion.125, bf16[192,32,256]{2,1,0:T(8,128)(2,1)S(1)} %copy.209), kind=kOutput, calls=%fused_computation.104 | convolution fusion | flops 4843765760 | bytes 47185920 | tf_op jit(solution)/shard_map/cwh,kh->cwk/dot_general | solution.py:49
  263.3 10.9 fusion.121
  294.3 11.0 fusion.117
  338.3 32.8 %collective-permute-done = bf16[192,32,32]{0,2,1:T(8,128)(2,1)} collective-permute-done((bf16[192,32,32]{0,2,1:T(8,128)(2,1)}, bf16[192,32,32]{0,2,1:T(8,128)(2,1)}, u32[]{:S(2)}, u32[]{:S(2)}) %collective-permute-start) | collective-permute-done | bytes 393248 | tf_op jit(solution)/shard_map/ppermute | solution.py:30
  382.3 62.4 %collective-permute-start.6 = (bf16[192,32,32]{0,2,1:T(8,128)(2,1)}, bf16[192,32,32]{0,2,1:T(8,128)(2,1)S(1)}, u32[]{:S(2)}, u32[]{:S(2)}) collective-permute-start(bf16[192,32,32]{0,2,1:T(8,128)(2,1)} %get-tuple-element.26), channel_id=1, source_target_pairs={{0,28},{4,0},{8,4},{12,8},{16,12},{20,16},{24,20},{28,24},{1,29},{... | collective-permute-start | bytes 1179656 | tf_op jit(solution)/shard_map/ppermute | solution.py:30
  447.3 27.6 %collective-permute-done.3 = bf16[192,32,32]{0,2,1:T(8,128)(2,1)S(1)} collective-permute-done((bf16[192,32,32]{0,2,1:T(8,128)(2,1)}, bf16[192,32,32]{0,2,1:T(8,128)(2,1)S(1)}, u32[]{:S(2)}, u32[]{:S(2)}) %collective-permute-start.3) | collective-permute-done | bytes 393248 | tf_op jit(solution)/shard_map/ppermute | solution.py:30
  535.2 37.9 %fusion.255 = (bf16[192,32,256]{2,1,0:T(8,128)(2,1)S(1)}, f32[192,32,256]{2,1,0:T(8,128)}) fusion(f32[192]{0:T(256)S(1)} %bitcast.374, f32[192,34,256]{2,1,0:T(8,128)} %maximum_convert_fusion, f32[192]{0:T(256)S(1)} %bitcast.376, f32[192]{0:T(256)S(1)} %bitcast.362, f32[192]{0:T(256)S(1)} %bitcast.364, f32[192]{0:T(256)S(1)} %bitcast.366, ...), kind=kLoop, calls=%fused_computation.331 | loop fusion | flops 31457280 | bytes 39328512 | tf_op jit(solution)/shard_map/convert_element_type | solution.py:147
  599.7 9.7 reshape.176
  609.4 15.8 %fusion.263 = f32[3072,2048]{0,1} fusion(bf16[3072,768]{1,0:T(8,128)(2,1)} %all-gather.5.cloned.1.call-done, bf16[768,2048]{0,1:T(8,128)(2,1)S(1)} %reshape.206), kind=kOutput, calls=%fused_computation.336 | convolution fusion | flops 9663676416 | bytes 33030144
  641.2 13.8 copy.220
  655.0 10.2 reshape.179
  673.6 79.9 %fusion.7 = (bf16[3072,32,64]{0,2,1:T(8,128)(2,1)}, bf16[3072,32,64]{0,2,1:T(8,128)(2,1)}) fusion(f32[3072,32,64]{0,2,1:T(8,128)} %bitcast.379, bf16[768,3072]{1,0:T(8,128)(2,1)S(1)} %bitcast.358, f32[768,32,64]{0,2,1:T(8,128)S(1)} %subtract_multiply_fusion, f32[768]{0:T(1024)S(1)} %copy-done.32), kind=kOutput, calls=%fused_computation.11 | convolution fusion | flops 10138681344 | bytes 61344768 | tf_op jit(solution)/shard_map/chw,cf->fhw/dot_general | solution.py:158
  753.6 22.7 %bitcast_reduce_fusion = (f32[4,32,64]{2,1,0:T(8,128)S(1)}, f32[4,32,64]{2,1,0:T(8,128)S(1)}, f32[4,32,64,768]{3,2,1,0:T(8,128)}) fusion(f32[768]{0:T(1024)S(1)} %copy-done.32, f32[768,32,64]{0,2,1:T(8,128)} %copy-done.8, bf16[768,4,768,1]{2,1,0,3:T(4,128)(2,1)} %bitcast.359, bf16[32,8,4,8,768]{4,3,2,1,0:T(8,128)(2,1)} %bitcast.381), kind=kOutput, calls=%fused_computation.14 | convolution fusion | flops 9688825856 | bytes 48827392 | tf_op jit(solution)/shard_map/pjra,spj->psra/dot_general | solution.py:172
  776.3 16.1 %fusion.10 = bf16[4,768,32,64]{1,3,2,0:T(8,128)(2,1)} fusion(f32[4,32,64,768]{3,2,1,0:T(8,128)} %get-tuple-element.47, f32[4,32,64]{2,1,0:T(8,128)S(1)} %get-tuple-element.48, f32[768,32,64]{0,2,1:T(8,128)} %copy-done.8, f32[4,32,64]{2,1,0:T(8,128)S(1)} %get-tuple-element.49, f32[768]{0:T(1024)S(1)} %copy-done.32, f32[32,64]{1,0:T(8,128)S(1)} %copy-done.11), kind=kLoop, calls=%fused_computation.17 | loop fusion | flops 37748736 | bytes 44116992 | tf_op jit(solution)/shard_map/convert_element_type | solution.py:129
  799.7 9.8 copy.231
  816.1 40.3 %all_to_all.153 = bf16[4,2,196608]{2,1,0:T(2,128)(2,1)} all-to-all(bf16[4,2,196608]{2,1,0:T(2,128)(2,1)S(1)} %reshape.212), channel_id=1, replica_groups=mesh['rows'=8,'ch'=4] {'ch'}, dimensions={0} | all-to-all | bytes 6291456 | tf_op jit(solution)/shard_map/all_to_all | solution.py:138
  914.9 15.1 %fusion.57 = f32[192,32,256]{2,1,0:T(8,128)} fusion(f32[192,34,256]{2,1,0:T(8,128)S(1)} %maximum_convert_fusion.1, f32[192]{0:T(256)S(1)} %bitcast.375, f32[192]{0:T(256)S(1)} %bitcast.377, f32[192]{0:T(256)S(1)} %bitcast.363, f32[192]{0:T(256)S(1)} %bitcast.365, f32[192]{0:T(256)S(1)} %bitcast.367, f32[192]{0:T(256)S(1)} %bitcast.369, f32[192]{0:T(256)S(1)} %bitcast.371, ...), kind=kLoop, calls=%fused_computation.88 | loop fusion | flops 26738688 | bytes 33039360 | tf_op jit(solution)/shard_map/add | solution.py:100
  930.0 12.5 fusion.77
  957.4 12.5 convert_bitcast_fusion.2
  975.6 73.4 %all-to-all-done.8 = bf16[192,256,32]{0,2,1:T(8,128)(2,1)} async-done(((bf16[192,256,32]{0,2,1:T(8,128)(2,1)}), bf16[192,256,32]{0,2,1:T(8,128)(2,1)}, u32[]{:S(2)}, u32[]{:S(2)}) %all-to-all-start.8) | async-done | bytes 3145760 | tf_op jit(solution)/shard_map/all_to_all | solution.py:70
  1054.9 17.0 %convert_bitcast_fusion = bf16[4,768,32,64]{1,3,2,0:T(8,128)(2,1)} fusion(bf16[4,768,768,1]{2,1,3,0:T(8,128)(2,1)} %bitcast.378, bf16[32,8,4,8,768]{4,3,2,1,0:T(8,128)(2,1)} %bitcast.380), kind=kOutput, calls=%fused_computation.62 | convolution fusion | flops 9669967872 | bytes 29884416 | tf_op jit(solution)/shard_map/bfhw,bfc->bchw/dot_general | solution.py:161
  1113.8 32.7 %all-to-all-done.7 = bf16[192,256,32]{0,2,1:T(8,128)(2,1)} async-done(((bf16[192,256,32]{0,2,1:T(8,128)(2,1)}), bf16[192,256,32]{0,2,1:T(8,128)(2,1)}, u32[]{:S(2)}, u32[]{:S(2)}) %all-to-all-start.7) | async-done | bytes 3145760 | tf_op jit(solution)/shard_map/all_to_all | solution.py:67
  1182.2 23.1 %multiply_bitcast_fusion.1 = (f32[1,192,32,256]{3,2,1,0:T(8,128)}, f32[1,192,32,256]{3,2,1,0:T(8,128)}, f32[192,32,256]{2,1,0:T(8,128)}, f32[192,32,256]{2,1,0:T(8,128)}) fusion(f32[192,32,256]{2,1,0:T(8,128)} %convolution_subtract_fusion, f32[192,32,256]{2,1,0:T(8,128)S(1)} %bitcast.334, f32[192,32,256]{2,1,0:T(8,128)} %get-tuple-element.46, ...), kind=kOutput, calls=%fused_computation.112 | convolution fusion | flops 4857921536 | bytes 66060288 | tf_op jit(solution)/shard_map/cwh,kh->cwk/dot_general | solution.py:49
  1205.3 11.1 fusion.110
  1284.6 10.7 fusion.106
  1318.7 12.1 pad_maximum_fusion
  1337.9 11.1 collective-permute-done.12
  1349.0 38.2 %collective-permute-start.17 = (bf16[192,32,32]{0,2,1:T(8,128)(2,1)S(1)}, bf16[192,32,32]{0,2,1:T(8,128)(2,1)S(1)}, u32[]{:S(2)}, u32[]{:S(2)}) collective-permute-start(bf16[192,32,32]{0,2,1:T(8,128)(2,1)S(1)} %get-tuple-element.17), channel_id=1, source_target_pairs={{0,28},{4,0},{8,4},{12,8},{16,12},{20,16},{24,20},{28,24},{1,29},{... | collective-permute-start | bytes 1179656 | tf_op jit(solution)/shard_map/ppermute | solution.py:30
  1388.8 29.7 %collective-permute-done.14 = bf16[192,32,32]{0,2,1:T(8,128)(2,1)S(1)} collective-permute-done((bf16[192,32,32]{0,2,1:T(8,128)(2,1)S(1)}, bf16[192,32,32]{0,2,1:T(8,128)(2,1)S(1)}, u32[]{:S(2)}, u32[]{:S(2)}) %collective-permute-start.14) | collective-permute-done | bytes 393248 | tf_op jit(solution)/shard_map/ppermute | solution.py:30
  (233 shorter events, 575.4 us)
Async XLA Ops:
  24.9 97.6 %all-to-all-start.1 = ((bf16[192,256,32]{0,2,1:T(8,128)(2,1)}), bf16[192,256,32]{0,2,1:T(8,128)(2,1)}, u32[]{:S(2)}, u32[]{:S(2)}) async-start(bf16[192,256,32]{0,2,1:T(8,128)(2,1)} %copy.207), calls=%async_computation.1 | async-start | bytes 8388608 | tf_op jit(solution)/shard_map/all_to_all | solution.py:70
  122.5 97.1 %all-to-all-start = ((bf16[192,256,32]{0,2,1:T(8,128)(2,1)}), bf16[192,256,32]{0,2,1:T(8,128)(2,1)}, u32[]{:S(2)}, u32[]{:S(2)}) async-start(bf16[192,256,32]{0,2,1:T(8,128)(2,1)} %copy.203), calls=%async_computation | async-start | bytes 8388608 | tf_op jit(solution)/shard_map/all_to_all | solution.py:67
  127.9 471.7 %all-gather.3.cloned.1.call-start = ((), (), s32[]{:S(2)}) async-start(), calls=%async_computation.10 | async-start | bytes 5898240 | tf_op jit(solution)/shard_map/all_gather | solution.py:150
  288.0 202.8 %all-to-all-start.2 = ((bf16[192,32,256]{0,1,2:T(8,128)(2,1)}), bf16[192,32,256]{0,1,2:T(8,128)(2,1)}, u32[]{:S(2)}, u32[]{:S(2)}) async-start(bf16[192,32,256]{0,1,2:T(8,128)(2,1)} %copy.212), calls=%async_computation.2 | async-start | bytes 8388608 | tf_op jit(solution)/shard_map/all_to_all | solution.py:83
  293.4 316.0 %all-gather.5.cloned.1.call-start = ((), (), s32[]{:S(2)}) async-start(), calls=%async_computation.11 | async-start | bytes 5898240 | tf_op jit(solution)/shard_map/all_gather | solution.py:151
  325.1 46.0 %collective-permute-start = (bf16[192,32,32]{0,2,1:T(8,128)(2,1)}, bf16[192,32,32]{0,2,1:T(8,128)(2,1)}, u32[]{:S(2)}, u32[]{:S(2)}) collective-permute-start(bf16[192,32,32]{0,2,1:T(8,128)(2,1)} %get-tuple-element.32), channel_id=1, source_target_pairs={{0,4},{4,8},{8,12},{12,16},{16,20},{20,24},{24,28},{28,0},{1,5},{5... | collective-permute-start | bytes 1179656 | tf_op jit(solution)/shard_map/ppermute | solution.py:30
  325.1 57.2 %collective-permute-start.1 = (bf16[192,32,32]{0,2,1:T(8,128)(2,1)}, bf16[192,32,32]{0,2,1:T(8,128)(2,1)}, u32[]{:S(2)}, u32[]{:S(2)}) collective-permute-start(bf16[192,32,32]{0,2,1:T(8,128)(2,1)} %get-tuple-element.31), channel_id=1, source_target_pairs={{0,8},{4,12},{8,16},{12,20},{16,24},{20,28},{24,0},{28,4},{1,9},{5... | collective-permute-start | bytes 1179656 | tf_op jit(solution)/shard_map/ppermute | solution.py:30
  326.6 151.6 %copy-start.30 = (s32[1024]{0:T(1024)}, s32[1024]{0:T(1024)S(1)}, u32[]{:S(2)}) copy-start(s32[1024]{0:T(1024)S(1)} %pad_clamp_fusion) | copy-start | bytes 12292
  332.8 113.7 %collective-permute-start.2 = (bf16[192,32,32]{0,2,1:T(8,128)(2,1)}, bf16[192,32,32]{0,2,1:T(8,128)(2,1)S(1)}, u32[]{:S(2)}, u32[]{:S(2)}) collective-permute-start(bf16[192,32,32]{0,2,1:T(8,128)(2,1)} %get-tuple-element.30), channel_id=1, source_target_pairs={{0,12},{4,16},{8,20},{12,24},{16,28},{20,0},{24,4},{28,8},{1,13},{... | collective-permute-start | bytes 1179656 | tf_op jit(solution)/shard_map/ppermute | solution.py:30
  334.0 140.9 %collective-permute-start.3 = (bf16[192,32,32]{0,2,1:T(8,128)(2,1)}, bf16[192,32,32]{0,2,1:T(8,128)(2,1)S(1)}, u32[]{:S(2)}, u32[]{:S(2)}) collective-permute-start(bf16[192,32,32]{0,2,1:T(8,128)(2,1)} %get-tuple-element.29), channel_id=1, source_target_pairs={{0,16},{4,20},{8,24},{12,28},{16,0},{20,4},{24,8},{28,12},{1,17},{... | collective-permute-start | bytes 1179656 | tf_op jit(solution)/shard_map/ppermute | solution.py:30
  335.2 140.5 %collective-permute-start.4 = (bf16[192,32,32]{0,2,1:T(8,128)(2,1)}, bf16[192,32,32]{0,2,1:T(8,128)(2,1)S(1)}, u32[]{:S(2)}, u32[]{:S(2)}) collective-permute-start(bf16[192,32,32]{0,2,1:T(8,128)(2,1)} %get-tuple-element.28), channel_id=1, source_target_pairs={{0,20},{4,24},{8,28},{12,0},{16,4},{20,8},{24,12},{28,16},{1,21},{... | collective-permute-start | bytes 1179656 | tf_op jit(solution)/shard_map/ppermute | solution.py:30
  371.0 105.5 %collective-permute-start.5 = (bf16[192,32,32]{0,2,1:T(8,128)(2,1)}, bf16[192,32,32]{0,2,1:T(8,128)(2,1)S(1)}, u32[]{:S(2)}, u32[]{:S(2)}) collective-permute-start(bf16[192,32,32]{0,2,1:T(8,128)(2,1)} %get-tuple-element.27), channel_id=1, source_target_pairs={{0,24},{4,28},{8,0},{12,4},{16,8},{20,12},{24,16},{28,20},{1,25},{... | collective-permute-start | bytes 1179656 | tf_op jit(solution)/shard_map/ppermute | solution.py:30
  382.3 95.1 %collective-permute-start.6 = (bf16[192,32,32]{0,2,1:T(8,128)(2,1)}, bf16[192,32,32]{0,2,1:T(8,128)(2,1)S(1)}, u32[]{:S(2)}, u32[]{:S(2)}) collective-permute-start(bf16[192,32,32]{0,2,1:T(8,128)(2,1)} %get-tuple-element.26), channel_id=1, source_target_pairs={{0,28},{4,0},{8,4},{12,8},{16,12},{20,16},{24,20},{28,24},{1,29},{... | collective-permute-start | bytes 1179656 | tf_op jit(solution)/shard_map/ppermute | solution.py:30
  490.8 88.7 %all-to-all-start.5 = ((bf16[192,32,256]{0,1,2:T(8,128)(2,1)}), bf16[192,32,256]{0,1,2:T(8,128)(2,1)}, u32[]{:S(2)}, u32[]{:S(2)}) async-start(bf16[192,32,256]{0,1,2:T(8,128)(2,1)} %copy.226), calls=%async_computation.5 | async-start | bytes 8388608 | tf_op jit(solution)/shard_map/all_to_all | solution.py:134
  521.2 9.6 collective-permute-start.8
  522.5 8.3 collective-permute-start.7
  524.3 48.8 %copy-start.12 = (f32[192,1]{0,1:T(1,128)}, f32[192,1]{0,1:T(1,128)S(1)}, u32[]{:S(2)}) copy-start(f32[192,1]{0,1:T(1,128)S(1)} %get-tuple-element.37) | copy-start | bytes 2308
  579.4 52.2 %all-to-all-start.3 = ((bf16[192,32,256]{0,1,2:T(8,128)(2,1)}), bf16[192,32,256]{0,1,2:T(8,128)(2,1)}, u32[]{:S(2)}, u32[]{:S(2)}) async-start(bf16[192,32,256]{0,1,2:T(8,128)(2,1)} %copy.218), calls=%async_computation.3 | async-start | bytes 8388608 | tf_op jit(solution)/shard_map/all_to_all | solution.py:134
  673.6 80.0 %copy-start.8 = (f32[768,32,64]{0,2,1:T(8,128)}, f32[768,32,64]{0,2,1:T(8,128)S(1)}, u32[]{:S(2)}) copy-start(f32[768,32,64]{0,2,1:T(8,128)S(1)} %subtract_multiply_fusion) | copy-start | bytes 18874372
  900.7 7.7 collective-permute-start.10
  904.8 7.5 collective-permute-start.9
  948.2 100.8 %all-to-all-start.8 = ((bf16[192,256,32]{0,2,1:T(8,128)(2,1)}), bf16[192,256,32]{0,2,1:T(8,128)(2,1)}, u32[]{:S(2)}, u32[]{:S(2)}) async-start(bf16[192,256,32]{0,2,1:T(8,128)(2,1)} %copy.240), calls=%async_computation.8 | async-start | bytes 8388608 | tf_op jit(solution)/shard_map/all_to_all | solution.py:70
  1049.0 97.5 %all-to-all-start.7 = ((bf16[192,256,32]{0,2,1:T(8,128)(2,1)}), bf16[192,256,32]{0,2,1:T(8,128)(2,1)}, u32[]{:S(2)}, u32[]{:S(2)}) async-start(bf16[192,256,32]{0,2,1:T(8,128)(2,1)} %copy.236), calls=%async_computation.7 | async-start | bytes 8388608 | tf_op jit(solution)/shard_map/all_to_all | solution.py:67
  1146.5 83.7 %all-to-all-start.4 = ((bf16[4,2,196608]{2,1,0:T(2,128)(2,1)}), bf16[4,2,196608]{2,1,0:T(2,128)(2,1)}, u32[]{:S(2)}, u32[]{:S(2)}) async-start(bf16[4,2,196608]{2,1,0:T(2,128)(2,1)} %reshape.210), calls=%async_computation.4 | async-start | bytes 6291456 | tf_op jit(solution)/shard_map/all_to_all | solution.py:138
  1230.2 205.4 %all-to-all-start.9 = ((bf16[192,32,256]{0,1,2:T(8,128)(2,1)}), bf16[192,32,256]{0,1,2:T(8,128)(2,1)}, u32[]{:S(2)}, u32[]{:S(2)}) async-start(bf16[192,32,256]{0,1,2:T(8,128)(2,1)} %copy.245), calls=%async_computation.9 | async-start | bytes 8388608 | tf_op jit(solution)/shard_map/all_to_all | solution.py:83
  1313.6 19.1 %collective-permute-start.11 = (bf16[192,32,32]{0,2,1:T(8,128)(2,1)S(1)}, bf16[192,32,32]{0,2,1:T(8,128)(2,1)S(1)}, u32[]{:S(2)}, u32[]{:S(2)}) collective-permute-start(bf16[192,32,32]{0,2,1:T(8,128)(2,1)S(1)} %get-tuple-element.23), channel_id=1, source_target_pairs={{0,4},{4,8},{8,12},{12,16},{16,20},{20,24},{24,28},{28,0},{1,5},{5... | collective-permute-start | bytes 1179656 | tf_op jit(solution)/shard_map/ppermute | solution.py:30
  1313.7 35.3 %collective-permute-start.12 = (bf16[192,32,32]{0,2,1:T(8,128)(2,1)S(1)}, bf16[192,32,32]{0,2,1:T(8,128)(2,1)S(1)}, u32[]{:S(2)}, u32[]{:S(2)}) collective-permute-start(bf16[192,32,32]{0,2,1:T(8,128)(2,1)S(1)} %get-tuple-element.22), channel_id=1, source_target_pairs={{0,8},{4,12},{8,16},{12,20},{16,24},{20,28},{24,0},{28,4},{1,9},{5... | collective-permute-start | bytes 1179656 | tf_op jit(solution)/shard_map/ppermute | solution.py:30
  1315.1 72.9 %collective-permute-start.13 = (bf16[192,32,32]{0,2,1:T(8,128)(2,1)S(1)}, bf16[192,32,32]{0,2,1:T(8,128)(2,1)S(1)}, u32[]{:S(2)}, u32[]{:S(2)}) collective-permute-start(bf16[192,32,32]{0,2,1:T(8,128)(2,1)S(1)} %get-tuple-element.21), channel_id=1, source_target_pairs={{0,12},{4,16},{8,20},{12,24},{16,28},{20,0},{24,4},{28,8},{1,13},{... | collective-permute-start | bytes 1179656 | tf_op jit(solution)/shard_map/ppermute | solution.py:30
  1316.3 102.3 %collective-permute-start.14 = (bf16[192,32,32]{0,2,1:T(8,128)(2,1)S(1)}, bf16[192,32,32]{0,2,1:T(8,128)(2,1)S(1)}, u32[]{:S(2)}, u32[]{:S(2)}) collective-permute-start(bf16[192,32,32]{0,2,1:T(8,128)(2,1)S(1)} %get-tuple-element.20), channel_id=1, source_target_pairs={{0,16},{4,20},{8,24},{12,28},{16,0},{20,4},{24,8},{28,12},{1,17},{... | collective-permute-start | bytes 1179656 | tf_op jit(solution)/shard_map/ppermute | solution.py:30
  1317.5 101.9 %collective-permute-start.15 = (bf16[192,32,32]{0,2,1:T(8,128)(2,1)S(1)}, bf16[192,32,32]{0,2,1:T(8,128)(2,1)S(1)}, u32[]{:S(2)}, u32[]{:S(2)}) collective-permute-start(bf16[192,32,32]{0,2,1:T(8,128)(2,1)S(1)} %get-tuple-element.19), channel_id=1, source_target_pairs={{0,20},{4,24},{8,28},{12,0},{16,4},{20,8},{24,12},{28,16},{1,21},{... | collective-permute-start | bytes 1179656 | tf_op jit(solution)/shard_map/ppermute | solution.py:30
  1332.7 87.5 %collective-permute-start.16 = (bf16[192,32,32]{0,2,1:T(8,128)(2,1)S(1)}, bf16[192,32,32]{0,2,1:T(8,128)(2,1)S(1)}, u32[]{:S(2)}, u32[]{:S(2)}) collective-permute-start(bf16[192,32,32]{0,2,1:T(8,128)(2,1)S(1)} %get-tuple-element.18), channel_id=1, source_target_pairs={{0,24},{4,28},{8,0},{12,4},{16,8},{20,12},{24,16},{28,20},{1,25},{... | collective-permute-start | bytes 1179656 | tf_op jit(solution)/shard_map/ppermute | solution.py:30
  1349.0 72.1 %collective-permute-start.17 = (bf16[192,32,32]{0,2,1:T(8,128)(2,1)S(1)}, bf16[192,32,32]{0,2,1:T(8,128)(2,1)S(1)}, u32[]{:S(2)}, u32[]{:S(2)}) collective-permute-start(bf16[192,32,32]{0,2,1:T(8,128)(2,1)S(1)} %get-tuple-element.17), channel_id=1, source_target_pairs={{0,28},{4,0},{8,4},{12,8},{16,12},{20,16},{24,20},{28,24},{1,29},{... | collective-permute-start | bytes 1179656 | tf_op jit(solution)/shard_map/ppermute | solution.py:30
  (40 other events, 759.8 us)
Sparse Core Ops, SparseCore 0:
  130.3 39.0 all-gather.2
  295.8 39.0 all-gather.4
